TPU v7x, 128 devices: a whole 4x4x4 slice. The times are simulated.
128 devices in a mesh: tab: 32 (over x, y, core), rep: 4 (over z).
Axes of the slice: x: 4, y: 4, z: 4, core: 2. Of those that a mesh axis runs over, the one named last changes fastest.
Arguments:
- pooled: bfloat16 [64, 16384, 128], P('tab', 'rep'), may hold values from -6 to 6
- widths: int32 [64], replicated, may hold values from 16 to 128, as said below
- placement: int32 [64], replicated, may hold values from 0 to 63, each once
- route: int32 [4, 4096], P('rep'), may hold values from 0 to 4095, each once within a row
- labels: int32 [4, 4096], P('rep'), may hold values 0 or 1
- proj: bfloat16 [64, 128, 32], replicated, may hold values from -0.5 to 0.5
- senet_in: float32 [64, 32], replicated, may hold values from -6 to 6
- senet_out: float32 [32, 64], replicated, may hold values from -1 to 1
- bilinear: float32 [32, 32], replicated, may hold values from -1 to 1
- w_first: bfloat16 [4096, 256], replicated, may hold values from -0.09375 to 0.09375
- w_second: bfloat16 [256, 256], replicated, may hold values from -0.75 to 0.75
- w_last: bfloat16 [256], replicated, may hold values from -0.375 to 0.375
Outputs:
- scores: float32 [4, 4096], P('rep', 'tab')
- d_pooled: bfloat16 [64, 16384, 128], P('tab', 'rep')
- d_proj: float32 [64, 128, 32], P('tab')
- d_senet_in: float32 [64, 32], replicated
- d_senet_out: float32 [32, 64], replicated
- d_bilinear: float32 [32, 32], replicated
- d_first: float32 [4096, 256], P('tab')
- d_second: float32 [256, 256], replicated
- d_last: float32 [256], replicated
Inputs may be any that keep to these rules, and one draw needn't show every extreme that they name: `widths`: each field's width is 128, 64, 32 or 16. `placement`: a permutation of the fields. `route`: each row is a permutation of 0 to 4095.
All inputs are finite; a program needn't handle non-finite values. No bound on the sum of `labels` on one device may be relied on, other than what follows from the above.
Results may differ from a plain program's by a relative error of at most 0.017.
Values may be sent and summed in bfloat16 or wider, within the bound.
A program may use at most 64 MiB of HBM per device.

v0:
```python
import jax
import jax.numpy as jnp
from jax import lax
from jax.sharding import PartitionSpec as P


def sent_to_all(value, axis):
    peers = lax.axis_size(axis)
    return lax.all_to_all(
        jnp.broadcast_to(value[None], (peers, *value.shape)), axis, 0, 0, tiled=True
    )


def of_everyone(value, axis):
    everything = sent_to_all(value, axis)
    return jnp.sum(everything.astype(jnp.float32), axis=0)


def laid_out(pieces, dim):
    lengths = list(pieces.shape[1:])
    lengths[dim] *= pieces.shape[0]
    return jnp.moveaxis(pieces, 0, dim).reshape(lengths)


def collect(value, axis, dim):
    pieces = sent_to_all(value, axis)
    return laid_out(pieces, dim)


def silu_slope(pre_act):
    logistic = jax.nn.sigmoid(pre_act)
    return logistic * (1.0 + pre_act * (1.0 - logistic))


def bilinear_forward(fields_in, bilinear, factor):
    product = jnp.einsum("fnc,cd->fnd", fields_in, bilinear)
    others = jnp.sum(fields_in, axis=0, keepdims=True) - fields_in
    return (product * others * factor, product, others)


def bilinear_backward(fields_in, product, others, upstream, bilinear, factor):
    d_product = upstream * others * factor
    d_others = upstream * product * factor
    d_fields = jnp.einsum("fnd,cd->fnc", d_product, bilinear)
    d_fields = d_fields + jnp.sum(d_others, axis=0, keepdims=True) - d_others
    d_weight = jnp.einsum("fnc,fnd->cd", fields_in, d_product)
    return (d_fields, d_weight)


def owner_pass(embeds, targets, senet_in, senet_out, bilinear, w_first, w_second, w_last):
    count = embeds.shape[0]
    width = embeds.shape[2]
    hidden = w_second.shape[0]
    factor = count ** (-0.5)
    first = w_first.reshape(2, count, width, hidden)
    dense = embeds.astype(jnp.float32)
    squeeze = jnp.mean(dense, axis=2)
    pre_one = jnp.einsum("fn,fr->rn", squeeze, senet_in)
    act_one = jax.nn.silu(pre_one)
    pre_two = jnp.einsum("rn,rf->fn", act_one, senet_out)
    weights = jax.nn.sigmoid(pre_two)
    scaled = weights[:, :, None] * dense
    plain_out, plain_prod, plain_rest = bilinear_forward(dense, bilinear, factor)
    scaled_out, scaled_prod, scaled_rest = bilinear_forward(scaled, bilinear, factor)
    joined = jnp.stack([plain_out, scaled_out]).astype(jnp.bfloat16)
    pre_hidden = jnp.einsum("kfnc,kfch->nh", joined, first, preferred_element_type=jnp.float32)
    hidden_one = jax.nn.silu(pre_hidden).astype(jnp.bfloat16)
    pre_second = jnp.dot(hidden_one, w_second, preferred_element_type=jnp.float32)
    hidden_two = jax.nn.silu(pre_second).astype(jnp.bfloat16)
    logits = jnp.dot(hidden_two, w_last, preferred_element_type=jnp.float32)
    grad_logit = jax.nn.sigmoid(logits) - targets
    d_last = jnp.dot(grad_logit, hidden_two.astype(jnp.float32))
    last_wide = w_last.astype(jnp.float32)
    d_pre_two = (grad_logit[:, None] * last_wide[None, :] * silu_slope(pre_second)).astype(
        jnp.bfloat16
    )
    d_second = jnp.dot(hidden_one.T, d_pre_two, preferred_element_type=jnp.float32)
    back_two = jnp.dot(d_pre_two, w_second.T, preferred_element_type=jnp.float32)
    d_pre_one = (back_two * silu_slope(pre_hidden)).astype(jnp.bfloat16)
    d_first = jnp.einsum(
        "kfnc,nh->kfch", joined, d_pre_one, preferred_element_type=jnp.float32
    ).reshape(-1, hidden)
    d_joined = jnp.einsum("nh,kfch->kfnc", d_pre_one, first, preferred_element_type=jnp.float32)
    d_plain, d_bil_plain = bilinear_backward(
        dense, plain_prod, plain_rest, d_joined[0], bilinear, factor
    )
    d_scaled, d_bil_scaled = bilinear_backward(
        scaled, scaled_prod, scaled_rest, d_joined[1], bilinear, factor
    )
    d_weights = jnp.sum(d_scaled * dense, axis=2)
    d_pre_w = d_weights * weights * (1.0 - weights)
    d_senet_out = jnp.einsum("rn,fn->rf", act_one, d_pre_w)
    d_act = jnp.einsum("fn,rf->rn", d_pre_w, senet_out) * silu_slope(pre_one)
    d_senet_in = jnp.einsum("fn,rn->fr", squeeze, d_act)
    d_squeeze = jnp.einsum("rn,fr->fn", d_act, senet_in)
    d_embeds = d_plain + weights[:, :, None] * d_scaled + d_squeeze[:, :, None] / width
    small = (d_senet_in, d_senet_out, d_bil_plain + d_bil_scaled, d_second, d_last)
    return (logits, d_embeds.astype(jnp.bfloat16), small, d_first, joined, d_pre_one)


def shards(
    pooled,
    widths,
    placement,
    route,
    labels,
    proj,
    senet_in,
    senet_out,
    bilinear,
    w_first,
    w_second,
    w_last,
):
    tab_count = lax.axis_size("tab")
    tab_index = lax.axis_index("tab")
    local_count = pooled.shape[0]
    rep_rows = pooled.shape[1]
    padded = pooled.shape[2]
    field_count = placement.shape[0]
    owner_rows = rep_rows // tab_count
    field_ids = jnp.arange(field_count, dtype=jnp.int32)
    matches = placement[:, None] == field_ids[None, :]
    slot_width = jnp.sum(jnp.where(matches, widths[None, :], 0), axis=1)
    slot_mask = (jnp.arange(padded, dtype=jnp.int32)[None, :] < slot_width[:, None]).astype(
        jnp.bfloat16
    )
    inverse = jnp.zeros_like(placement).at[placement].set(field_ids)
    targets = lax.dynamic_slice_in_dim(labels[0], tab_index * owner_rows, owner_rows).astype(
        jnp.float32
    )
    first_slot = tab_index * local_count
    local_fields = lax.dynamic_slice_in_dim(placement, first_slot, local_count)
    local_mask = lax.dynamic_slice_in_dim(slot_mask, first_slot, local_count, 0)
    local_proj = jnp.take(proj, local_fields, axis=0)
    masked = pooled * local_mask[:, None, :]
    embed_local = jnp.einsum(
        "fnc,fcd->fnd", masked, local_proj, preferred_element_type=jnp.float32
    ).astype(jnp.bfloat16)
    embed_slot = lax.all_to_all(embed_local, "tab", split_axis=1, concat_axis=0, tiled=True)
    logits, d_embeds, small, d_first_part, joined, d_pre_one = owner_pass(
        embed_slot[inverse], targets, senet_in, senet_out, bilinear, w_first, w_second, w_last
    )
    d_slot = d_embeds[placement]
    d_local = lax.all_to_all(d_slot, "tab", split_axis=0, concat_axis=1, tiled=True)
    back = jnp.einsum("fnd,fcd->fnc", d_local, local_proj, preferred_element_type=jnp.float32)
    back = (back * local_mask[:, None, :]).astype(jnp.bfloat16)
    d_proj_part = jnp.einsum("fnc,fnd->fcd", masked, d_local, preferred_element_type=jnp.float32)
    d_proj = of_everyone(d_proj_part.astype(jnp.bfloat16), "rep").astype(jnp.float32)
    first_tab = lax.psum_scatter(
        d_first_part.astype(jnp.bfloat16), "tab", scatter_dimension=0, tiled=True
    )
    d_first = of_everyone(first_tab, "rep").astype(jnp.float32)
    part_in, part_out, part_bil, part_second, part_last = small
    d_senet_in, d_senet_out, d_bilinear, d_second, d_last = lax.psum(
        (part_in, part_out, part_bil, part_second, part_last), ("tab", "rep")
    )
    all_logits = collect(logits, "tab", 0)
    wanted = lax.dynamic_slice_in_dim(route[0], tab_index * owner_rows, owner_rows)
    scores = jnp.take(all_logits, wanted)[None, :]
    return (scores, back, d_proj, d_senet_in, d_senet_out, d_bilinear, d_first, d_second, d_last)


def solution(mesh):
    placed = (
        P("tab", "rep", None),
        P(),
        P(),
        P("rep", None),
        P("rep", None),
        P(),
        P(),
        P(),
        P(),
        P(),
        P(),
        P(),
    )
    return jax.shard_map(
        shards,
        mesh=mesh,
        in_specs=placed,
        out_specs=(
            P("rep", "tab"),
            P("tab", "rep", None),
            P("tab", None, None),
            P(),
            P(),
            P(),
            P("tab", None),
            P(),
            P(),
        ),
        check_vma=False,
    )
```

profile of v0, /device:TPU:1, one launch (start us, length us, event | category | flops | bytes accessed | tf_op | source)
XLA Modules:
  0.0 225.5 jit_solution(7572727441180644628)
XLA Ops:
  8.0 1.0 select_reduce_fusion
  9.0 0.7 compare_and_fusion
  9.9 1.6 gather_fusion
  11.5 2.4 %convolution_convert_fusion = bf16[2,4096,32]{1,2,0:T(8,128)(2,1)S(1)} fusion(bf16[2,4096,128]{2,1,0:T(8,128)(2,1)} %param.12, bf16[2,128]{1,0:T(2,128)(2,1)S(1)} %get-tuple-element.22, bf16[2,128,32]{1,2,0:T(8,128)(2,1)S(1)} %gather_fusion, pred[2]{0:T(512)(128)(4,1)S(1)} %get-tuple-element.17), kind=kOutput, calls=%fused_computation.7 | convolution fusion | flops 68427776 | bytes 2638338 | tf_op jit(solution)/shard_map/fnc,fcd->fnd/dot_general | solution.py:137
  14.0 3.8 %copy.56 = bf16[2,4096,32]{2,0,1:T(2,128)(2,1)} copy(bf16[2,4096,32]{1,2,0:T(8,128)(2,1)S(1)} %convolution_convert_fusion) | data formatting | bytes 1048576 | tf_op jit(solution)/shard_map/convert_element_type | solution.py:139
  17.8 5.9 %reshape.152 = bf16[32,2,4096]{2,1,0:T(2,128)(2,1)} reshape(bf16[4096,2,32]{2,1,0:T(2,128)(2,1)} %bitcast.166) | data formatting | bytes 1048576
  23.7 8.6 %all-to-all-start = ((bf16[32,2,4096]{2,1,0:T(2,128)(2,1)}), bf16[32,2,4096]{2,1,0:T(2,128)(2,1)S(1)}, u32[]{:S(2)}, u32[]{:S(2)}) async-start(bf16[32,2,4096]{2,1,0:T(2,128)(2,1)} %reshape.152), calls=%async_computation | async-start | bytes 1048576 | tf_op jit(solution)/shard_map/all_to_all | solution.py:140
  32.4 0.8 scatter_custom_fusion
  33.2 10.7 %all-to-all-done = bf16[32,2,4096]{2,1,0:T(2,128)(2,1)S(1)} async-done(((bf16[32,2,4096]{2,1,0:T(2,128)(2,1)}), bf16[32,2,4096]{2,1,0:T(2,128)(2,1)S(1)}, u32[]{:S(2)}, u32[]{:S(2)}) %all-to-all-start) | async-done | bytes 524320 | tf_op jit(solution)/shard_map/all_to_all | solution.py:140
  43.9 2.0 reshape.153
  45.8 4.7 %copy.73 = bf16[2,32,128,32]{2,3,0,1:T(8,128)(2,1)S(1)} copy(bf16[2,32,128,32]{3,0,2,1:T(2,128)(2,1)} %bitcast.167) | data formatting | bytes 1048576 | tf_op jit(solution)/shard_map/all_to_all | solution.py:140
  50.5 0.7 gather_fusion.1
  51.9 0.3 fusion.9
  52.2 0.3 fusion.106
  52.6 0.4 fusion.49
  53.2 0.5 fusion.19
  53.8 0.4 copy-done.9
  54.3 0.8 divide_subtract_fusion
  55.4 2.0 convolution_convert_fusion.1
  57.4 0.7 fusion.82
  58.1 0.6 broadcast_in_dim.45
  58.7 3.6 %all-to-all-start.1 = ((f32[32,1,128]{2,1,0:T(1,128)}), f32[32,1,128]{2,1,0:T(1,128)S(1)}, u32[]{:S(2)}, u32[]{:S(2)}) async-start(f32[32,1,128]{2,1,0:T(1,128)} %broadcast_in_dim.45), calls=%async_computation.1 | async-start | bytes 32768 | tf_op jit(solution)/shard_map/all_to_all | solution.py:9
  62.4 0.7 convolution_bitcast_fusion
  63.2 0.3 convolution_bitcast_fusion.1
  63.5 1.7 copy-done.3
  65.1 0.3 copy-done.5
  65.4 0.5 fusion.66
  66.0 1.5 fusion.41
  68.1 1.0 fusion.99
  69.1 2.7 %fusion.14 = bf16[64,128,32]{1,2,0:T(8,128)(2,1)S(1)} fusion(f32[64,128,32]{1,2,0:T(8,128)} %get-tuple-element.28, bf16[64,128,32]{1,2,0:T(8,128)(2,1)S(1)} %gather_fusion.1, f32[2,64,128,32]{2,3,1,0:T(8,128)} %copy-done.1, f32[64,128]{1,0:T(8,128)S(1)} %fusion.24, f32[128,32]{0,1:T(8,128)S(1)} %get-tuple-element.9, f32[64,128]{1,0:T(8,128)S(1)} %fusion.28, ...), kind=kOutput, calls=%fused_computation.30 | convolution fusion | flops 19922944 | bytes 5345280 | tf_op jit(solution)/shard_map/fnd,cd->fnc/dot_general | solution.py:44
  71.8 1.4 gather_fusion.3
  73.2 7.4 %all-to-all-start.2 = ((bf16[64,128,32]{1,2,0:T(8,128)(2,1)}), bf16[64,128,32]{1,2,0:T(8,128)(2,1)S(1)}, u32[]{:S(2)}, u32[]{:S(2)}) async-start(bf16[64,128,32]{1,2,0:T(8,128)(2,1)} %gather_fusion.3), calls=%async_computation.2 | async-start | bytes 1048576 | tf_op jit(solution)/shard_map/all_to_all | solution.py:145
  80.7 1.6 fusion.34
  82.4 68.8 %all-reduce = (f32[64,32]{0,1:T(8,128)}, f32[32,64]{1,0:T(8,128)}, f32[32,32]{1,0:T(8,128)}, f32[256]{0:T(256)}) all-reduce(f32[64,32]{0,1:T(8,128)S(1)} %fusion.68, f32[32,64]{1,0:T(8,128)S(1)} %fusion.79, f32[32,32]{1,0:T(8,128)S(1)} %fusion.34, f32[256]{0:T(256)S(1)} %bitcast.171), channel_id=1, replica_groups=mesh['tab'=32,'rep'=4] {'tab','rep'}, use_global_device_ids=true, to_apply=%region_9.10 | all-reduce | flops 5376 | bytes 43008 | tf_op jit(solution)/shard_map/psum | solution.py:155
  151.2 1.1 gather_fusion.2
  152.4 2.2 fusion.29
  154.5 0.6 broadcast_in_dim.49
  155.2 3.3 %all-to-all-start.3 = ((bf16[4,2,128,32]{2,3,1,0:T(8,128)(2,1)}), bf16[4,2,128,32]{2,3,1,0:T(8,128)(2,1)S(1)}, u32[]{:S(2)}, u32[]{:S(2)}) async-start(bf16[4,2,128,32]{2,3,1,0:T(8,128)(2,1)} %broadcast_in_dim.49), calls=%async_computation.3 | async-start | bytes 131072 | tf_op jit(solution)/shard_map/all_to_all | solution.py:9
  158.5 1.2 and_select_fusion
  159.7 3.3 %all-to-all-done.3 = bf16[4,2,128,32]{2,3,1,0:T(8,128)(2,1)S(1)} async-done(((bf16[4,2,128,32]{2,3,1,0:T(8,128)(2,1)}), bf16[4,2,128,32]{2,3,1,0:T(8,128)(2,1)S(1)}, u32[]{:S(2)}, u32[]{:S(2)}) %all-to-all-start.3) | async-done | bytes 65568 | tf_op jit(solution)/shard_map/all_to_all | solution.py:9
  162.9 1.6 broadcast_in_dim.82
  164.5 3.4 %all-to-all-start.4 = ((bf16[4,128,256]{2,1,0:T(8,128)(2,1)}), bf16[4,128,256]{2,1,0:T(8,128)(2,1)S(1)}, u32[]{:S(2)}, u32[]{:S(2)}) async-start(bf16[4,128,256]{2,1,0:T(8,128)(2,1)} %broadcast_in_dim.82), calls=%async_computation.5 | async-start | bytes 524288 | tf_op jit(solution)/shard_map/all_to_all | solution.py:9
  167.9 2.3 %fusion = bf16[2,4096,128]{2,1,0:T(8,128)(2,1)} fusion(f32[2,128]{1,0:T(2,128)S(1)} %get-tuple-element.21, bf16[32,2,4,8,128]{4,3,2,1,0:T(8,128)(2,1)S(1)} %bitcast.170, bf16[2,128,32]{1,2,0:T(8,128)(2,1)S(1)} %gather_fusion, pred[2]{0:T(512)(128)(4,1)S(1)} %get-tuple-element.17), kind=kOutput, calls=%fused_computation.6 | convolution fusion | flops 69214208 | bytes 2638850 | tf_op jit(solution)/shard_map/fnd,fcd->fnc/dot_general | solution.py:146
  170.1 0.6 convert_reduce_fusion.3
  170.8 2.6 %all-to-all-done.4 = bf16[4,128,256]{2,1,0:T(8,128)(2,1)S(1)} async-done(((bf16[4,128,256]{2,1,0:T(8,128)(2,1)}), bf16[4,128,256]{2,1,0:T(8,128)(2,1)S(1)}, u32[]{:S(2)}, u32[]{:S(2)}) %all-to-all-start.4) | async-done | bytes 262176 | tf_op jit(solution)/shard_map/all_to_all | solution.py:9
  173.4 0.7 convert_reduce_fusion.2
  174.1 42.3 %all-reduce.3.cloned.1.call-done = f32[256,256]{1,0:T(8,128)} async-done(((f32[256,256]{1,0:T(8,128)}), f32[256,256]{1,0:T(8,128)}) %all-reduce.3.cloned.1.call-update) | async-done | bytes 262160 | tf_op jit(solution)/shard_map/psum | solution.py:155
  216.3 1.7 copy.92
  (50 shorter events, 2.4 us)
Async XLA Ops:
  8.0 45.2 %copy-start = (bf16[4096,256]{1,0:T(8,128)(2,1)S(1)}, bf16[4096,256]{1,0:T(8,128)(2,1)}, u32[]{:S(2)}) copy-start(bf16[4096,256]{1,0:T(8,128)(2,1)} %param.21) | copy-start | bytes 6291460
  17.8 14.5 %copy-start.11 = (bf16[256]{0:T(256)(128)(2,1)S(1)}, bf16[256]{0:T(256)(128)(2,1)}, u32[]{:S(2)}) copy-start(bf16[256]{0:T(256)(128)(2,1)} %param.23) | copy-start | bytes 1540
  17.8 14.5 %copy-start.8 = (s32[64]{0:T(128)S(1)}, s32[64]{0:T(128)}, u32[]{:S(2)}) copy-start(s32[64]{0:T(128)} %param.14) | copy-start | bytes 772
  23.7 20.2 %all-to-all-start = ((bf16[32,2,4096]{2,1,0:T(2,128)(2,1)}), bf16[32,2,4096]{2,1,0:T(2,128)(2,1)S(1)}, u32[]{:S(2)}, u32[]{:S(2)}) async-start(bf16[32,2,4096]{2,1,0:T(2,128)(2,1)} %reshape.152), calls=%async_computation | async-start | bytes 1048576 | tf_op jit(solution)/shard_map/all_to_all | solution.py:140
  32.3 130.7 %reduce-scatter.2.cloned.1.call-start = ((), (), s32[]{:S(2)}) async-start(), calls=%async_computation.6 | async-start | bytes 2162688 | tf_op jit(solution)/shard_map/reduce_scatter | solution.py:150
  50.5 0.8 copy-start.7
  50.5 1.0 copy-start.10
  50.5 1.3 copy-start.6
  52.2 1.0 copy-start.4
  52.6 1.2 copy-start.2
  53.2 0.9 copy-start.9
  58.7 14.5 %all-to-all-start.1 = ((f32[32,1,128]{2,1,0:T(1,128)}), f32[32,1,128]{2,1,0:T(1,128)S(1)}, u32[]{:S(2)}, u32[]{:S(2)}) async-start(f32[32,1,128]{2,1,0:T(1,128)} %broadcast_in_dim.45), calls=%async_computation.1 | async-start | bytes 32768 | tf_op jit(solution)/shard_map/all_to_all | solution.py:9
  62.4 154.0 %all-reduce.3.cloned.1.call-start = ((), (), s32[]{:S(2)}) async-start(), calls=%async_computation.7 | async-start | bytes 524288 | tf_op jit(solution)/shard_map/psum | solution.py:155
  63.1 2.8 %copy-start.1 = (f32[2,64,128,32]{2,3,1,0:T(8,128)}, f32[2,64,128,32]{2,3,1,0:T(8,128)S(1)}, u32[]{:S(2)}) copy-start(f32[2,64,128,32]{2,3,1,0:T(8,128)S(1)} %convolution_bitcast_fusion) | copy-start | bytes 6291460
  63.1 2.0 copy-start.3
  63.1 2.3 %copy-start.5 = (f32[64,128,32]{1,2,0:T(8,128)S(1)}, f32[64,128,32]{1,2,0:T(8,128)}, u32[]{:S(2)}) copy-start(f32[64,128,32]{1,2,0:T(8,128)} %copy-done.4) | copy-start | bytes 3145732
  73.2 79.1 %all-to-all-start.2 = ((bf16[64,128,32]{1,2,0:T(8,128)(2,1)}), bf16[64,128,32]{1,2,0:T(8,128)(2,1)S(1)}, u32[]{:S(2)}, u32[]{:S(2)}) async-start(bf16[64,128,32]{1,2,0:T(8,128)(2,1)} %gather_fusion.3), calls=%async_computation.2 | async-start | bytes 1048576 | tf_op jit(solution)/shard_map/all_to_all | solution.py:145
  155.2 7.7 %all-to-all-start.3 = ((bf16[4,2,128,32]{2,3,1,0:T(8,128)(2,1)}), bf16[4,2,128,32]{2,3,1,0:T(8,128)(2,1)S(1)}, u32[]{:S(2)}, u32[]{:S(2)}) async-start(bf16[4,2,128,32]{2,3,1,0:T(8,128)(2,1)} %broadcast_in_dim.49), calls=%async_computation.3 | async-start | bytes 131072 | tf_op jit(solution)/shard_map/all_to_all | solution.py:9
  164.5 8.9 %all-to-all-start.4 = ((bf16[4,128,256]{2,1,0:T(8,128)(2,1)}), bf16[4,128,256]{2,1,0:T(8,128)(2,1)S(1)}, u32[]{:S(2)}, u32[]{:S(2)}) async-start(bf16[4,128,256]{2,1,0:T(8,128)(2,1)} %broadcast_in_dim.82), calls=%async_computation.5 | async-start | bytes 524288 | tf_op jit(solution)/shard_map/all_to_all | solution.py:9
Sparse Core Ops, SparseCore 0:
  57.6 75.3 reduce-scatter.1
Sparse Core Ops, SparseCore 1:
  69.2 147.1 all-reduce.2
where the time goes:
time: 226 us; the launch traced here: 225 us
  blocking collectives  68.8 us (30%)
  waiting for transfers between devices  58.9 us (26%)
  local copies, waits for them, and re-layouts  29.1 us (13%)
  starting transfers between devices  26.4 us (12%)
  matrix products  20.3 us (9%)
  between operations  15.8 us (7%)
  other arithmetic  6.22 us (3%)
    psum x1, blocking collectives, shards(): lax.psum((part_in, part_out, part_bil, part_second, part_last), ('tab', '...  68.8 us
    psum x1, waiting for transfers between devices, shards(): lax.psum((part_in, part_out, part_bil, part_second, part_last), ('tab', '...  42.3 us
    unnamed x28, local copies, waits for them, and re-layouts  12.1 us
    all_to_all x1, waiting for transfers between devices, shards(): lax.all_to_all(embed_local, 'tab', split_axis=1, concat_axis=0, tiled=True)  10.7 us
    all_to_all x3, starting transfers between devices, sent_to_all(): lax.all_to_all(jnp.broadcast_to(value[None], (peers, *value.shape)), axis...  10.3 us
    all_to_all x1, starting transfers between devices, shards(): lax.all_to_all(embed_local, 'tab', split_axis=1, concat_axis=0, tiled=True)  8.58 us
    all_to_all x1, starting transfers between devices, shards(): lax.all_to_all(d_slot, 'tab', split_axis=0, concat_axis=1, tiled=True)  7.39 us
    all_to_all x3, waiting for transfers between devices, sent_to_all(): lax.all_to_all(jnp.broadcast_to(value[None], (peers, *value.shape)), axis...  5.88 us
  transfers between devices with their start and end apart: 7, of which 4 were waited for; matrix products, arithmetic and copies ran while one was open for 10% of the time, Pallas kernels for 0%

commit v1 on v0

--- a/solution.py
+++ b/solution.py
@@ -2,6 +2,12 @@
 import jax.numpy as jnp
 from jax import lax
 from jax.sharding import PartitionSpec as P
+
+
+def _find_side(body, across, mesh_dim):
+    for dev in (across, mesh_dim):
+        body = jax.lax.psum(body, axis_name=dev)
+    return body
 
 
 def sent_to_all(value, axis):
@@ -152,8 +158,8 @@
     )
     d_first = of_everyone(first_tab, "rep").astype(jnp.float32)
     part_in, part_out, part_bil, part_second, part_last = small
-    d_senet_in, d_senet_out, d_bilinear, d_second, d_last = lax.psum(
-        (part_in, part_out, part_bil, part_second, part_last), ("tab", "rep")
+    d_senet_in, d_senet_out, d_bilinear, d_second, d_last = _find_side(
+        (part_in, part_out, part_bil, part_second, part_last), "tab", "rep"
     )
     all_logits = collect(logits, "tab", 0)
     wanted = lax.dynamic_slice_in_dim(route[0], tab_index * owner_rows, owner_rows)

time: 226 us -> 292 us (1.29)
  blocking collectives: 68.8 us -> 140 us
  waiting for transfers between devices: 58.9 us -> 53.7 us
    psum x1 -> x2, blocking collectives: 68.8 us -> 140 us  [_find_side(): body = jax.lax.psum(body, axis_name=dev)]
    psum x1 -> x2, waiting for transfers between devices: 42.3 us -> 31.5 us  [_find_side(): body = jax.lax.psum(body, axis_name=dev)]
    reduce_scatter x1, waiting for transfers between devices: 0.01 us -> 5.67 us  [shards(): lax.psum_scatter(d_first_part.astype(jnp.bfloat16), 'tab', scatter_dimens...]
    dot_general x2, matrix products: 4.24 us -> 1.09 us  [bilinear_backward(): d_fields = jnp.einsum('fnd,cd->fnc', d_product, bilinear)]
    unnamed x28 -> x32, local copies, waits for them, and re-layouts: 12.1 us -> 10.7 us
  transfers between devices with their start and end apart: 7 -> 8, of which waited for: 4 -> 6; matrix products, arithmetic and copies ran while one was open for 10% -> 9% of each run, Pallas kernels for 0% -> 0%
where the time goes in v1:
time: 292 us; the launch traced here: 290 us
  blocking collectives  140 us (48%)
  waiting for transfers between devices  53.7 us (18%)
  local copies, waits for them, and re-layouts  27.7 us (9%)
  starting transfers between devices  26.5 us (9%)
  matrix products  19.5 us (7%)
  between operations  14.1 us (5%)
  other arithmetic  8.5 us (3%)
    psum x2, blocking collectives, _find_side(): body = jax.lax.psum(body, axis_name=dev)  140 us
    psum x2, waiting for transfers between devices, _find_side(): body = jax.lax.psum(body, axis_name=dev)  31.5 us
    all_to_all x3, starting transfers between devices, sent_to_all(): lax.all_to_all(jnp.broadcast_to(value[None], (peers, *value.shape)), axis...  11 us
    unnamed x32, local copies, waits for them, and re-layouts  10.7 us
    all_to_all x1, waiting for transfers between devices, shards(): lax.all_to_all(embed_local, 'tab', split_axis=1, concat_axis=0, tiled=True)  9.99 us
    all_to_all x1, starting transfers between devices, shards(): lax.all_to_all(embed_local, 'tab', split_axis=1, concat_axis=0, tiled=True)  8.58 us
    all_to_all x1, starting transfers between devices, shards(): lax.all_to_all(d_slot, 'tab', split_axis=0, concat_axis=1, tiled=True)  6.76 us
    all_to_all x3, waiting for transfers between devices, sent_to_all(): lax.all_to_all(jnp.broadcast_to(value[None], (peers, *value.shape)), axis...  6.45 us
  transfers between devices with their start and end apart: 8, of which 6 were waited for; matrix products, arithmetic and copies ran while one was open for 9% of the time, Pallas kernels for 0%

profile of v1, /device:TPU:1, one launch (start us, length us, event | category | flops | bytes accessed | tf_op | source)
XLA Modules:
  0.0 289.8 jit_solution(15388546789475622234)
XLA Ops:
  7.2 1.0 select_reduce_fusion
  8.2 0.7 compare_and_fusion
  9.1 1.6 gather_fusion
  10.7 2.4 convolution_convert_fusion
  13.1 3.8 %copy.56 = bf16[2,4096,32]{2,0,1:T(2,128)(2,1)} copy(bf16[2,4096,32]{1,2,0:T(8,128)(2,1)S(1)} %convolution_convert_fusion) | data formatting | bytes 1048576 | tf_op jit(solution)/shard_map/convert_element_type | solution.py:145
  17.0 5.9 %reshape.152 = bf16[32,2,4096]{2,1,0:T(2,128)(2,1)} reshape(bf16[4096,2,32]{2,1,0:T(2,128)(2,1)} %bitcast.166) | data formatting | bytes 1048576
  22.8 8.6 %all-to-all-start = ((bf16[32,2,4096]{2,1,0:T(2,128)(2,1)}), bf16[32,2,4096]{2,1,0:T(2,128)(2,1)S(1)}, u32[]{:S(2)}, u32[]{:S(2)}) async-start(bf16[32,2,4096]{2,1,0:T(2,128)(2,1)} %reshape.152), calls=%async_computation | async-start | bytes 1048576 | tf_op jit(solution)/shard_map/all_to_all | solution.py:146
  31.6 0.8 scatter_custom_fusion
  32.3 0.7 fusion.82
  33.0 10.0 %all-to-all-done = bf16[32,2,4096]{2,1,0:T(2,128)(2,1)S(1)} async-done(((bf16[32,2,4096]{2,1,0:T(2,128)(2,1)}), bf16[32,2,4096]{2,1,0:T(2,128)(2,1)S(1)}, u32[]{:S(2)}, u32[]{:S(2)}) %all-to-all-start) | async-done | bytes 524320 | tf_op jit(solution)/shard_map/all_to_all | solution.py:146
  43.0 2.0 reshape.153
  45.0 4.7 %copy.73 = bf16[2,32,128,32]{2,3,0,1:T(8,128)(2,1)S(1)} copy(bf16[2,32,128,32]{3,0,2,1:T(2,128)(2,1)} %bitcast.167) | data formatting | bytes 1048576 | tf_op jit(solution)/shard_map/all_to_all | solution.py:146
  49.7 0.7 gather_fusion.1
  51.0 0.3 fusion.9
  51.4 0.3 fusion.106
  51.8 0.4 fusion.49
  52.4 0.5 fusion.19
  53.6 0.8 divide_subtract_fusion
  54.7 1.0 fusion.99
  55.7 3.1 %convolution_convert_fusion.1 = bf16[2,64,32,256]{3,2,1,0:T(8,128)(2,1)} fusion(bf16[128,256,1,1]{1,0,3,2:T(8,128)(2,1)S(1)} %fusion.23, bf16[1,64,128,32]{2,3,1,0:T(8,128)(2,1)} %copy-done.7, bf16[1,64,128,32]{2,3,1,0:T(8,128)(2,1)S(1)} %get-tuple-element.23), kind=kOutput, calls=%fused_computation.15 | convolution fusion | flops 270008320 | bytes 3211264 | tf_op jit(solution)/shard_map/kfnc,nh->kfch/dot_general | solution.py:86
  58.8 2.0 convolution_bitcast_fusion
  60.8 0.6 broadcast_in_dim.45
  61.4 3.6 %all-to-all-start.1 = ((f32[32,1,128]{2,1,0:T(1,128)}), f32[32,1,128]{2,1,0:T(1,128)S(1)}, u32[]{:S(2)}, u32[]{:S(2)}) async-start(f32[32,1,128]{2,1,0:T(1,128)} %broadcast_in_dim.45), calls=%async_computation.1 | async-start | bytes 32768 | tf_op jit(solution)/shard_map/all_to_all | solution.py:15
  65.1 2.8 fusion.66
  68.2 0.6 fusion.41
  69.3 0.5 fusion.14
  69.9 1.4 gather_fusion.3
  71.3 0.6 all-to-all-done.1
  72.0 6.8 %all-to-all-start.2 = ((bf16[64,128,32]{1,2,0:T(8,128)(2,1)}), bf16[64,128,32]{1,2,0:T(8,128)(2,1)S(1)}, u32[]{:S(2)}, u32[]{:S(2)}) async-start(bf16[64,128,32]{1,2,0:T(8,128)(2,1)} %gather_fusion.3), calls=%async_computation.2 | async-start | bytes 1048576 | tf_op jit(solution)/shard_map/all_to_all | solution.py:151
  78.9 1.7 convolution_bitcast_fusion.1
  80.6 0.4 fusion.34
  81.1 123.5 %all-reduce = (f32[64,32]{0,1:T(8,128)S(1)}, f32[32,64]{1,0:T(8,128)S(1)}, f32[32,32]{1,0:T(8,128)S(1)}, f32[256]{0:T(256)S(1)}) all-reduce(f32[64,32]{0,1:T(8,128)S(1)} %fusion.68, f32[32,64]{1,0:T(8,128)S(1)} %fusion.79, f32[32,32]{1,0:T(8,128)S(1)} %fusion.34, f32[256]{0:T(256)S(1)} %bitcast.171), channel_id=1, replica_groups=mesh['tab'=32,'rep'=4] {'tab'}, use_global_device_ids=true, to_apply=%region_9.10 | all-reduce | flops 5376 | bytes 43008 | tf_op jit(solution)/shard_map/psum | solution.py:9
  204.5 16.2 %all-reduce.1 = (f32[64,32]{0,1:T(8,128)}, f32[32,64]{1,0:T(8,128)}, f32[32,32]{1,0:T(8,128)}, f32[256]{0:T(256)}) all-reduce(f32[64,32]{0,1:T(8,128)S(1)} %get-tuple-element.13, f32[32,64]{1,0:T(8,128)S(1)} %get-tuple-element.14, f32[32,32]{1,0:T(8,128)S(1)} %get-tuple-element.15, ...), channel_id=1, replica_groups=mesh['tab'=32,'rep'=4] {'rep'}, use_global_device_ids=true, to_apply=%region_10.11 | all-reduce | flops 5376 | bytes 43008 | tf_op jit(solution)/shard_map/psum | solution.py:9
  220.7 1.1 gather_fusion.2
  221.9 2.2 fusion.29
  224.1 0.6 broadcast_in_dim.49
  224.7 3.3 %all-to-all-start.3 = ((bf16[4,2,128,32]{2,3,1,0:T(8,128)(2,1)}), bf16[4,2,128,32]{2,3,1,0:T(8,128)(2,1)S(1)}, u32[]{:S(2)}, u32[]{:S(2)}) async-start(bf16[4,2,128,32]{2,3,1,0:T(8,128)(2,1)} %broadcast_in_dim.49), calls=%async_computation.3 | async-start | bytes 131072 | tf_op jit(solution)/shard_map/all_to_all | solution.py:15
  228.1 1.2 and_select_fusion
  229.3 3.2 %all-to-all-done.3 = bf16[4,2,128,32]{2,3,1,0:T(8,128)(2,1)S(1)} async-done(((bf16[4,2,128,32]{2,3,1,0:T(8,128)(2,1)}), bf16[4,2,128,32]{2,3,1,0:T(8,128)(2,1)S(1)}, u32[]{:S(2)}, u32[]{:S(2)}) %all-to-all-start.3) | async-done | bytes 65568 | tf_op jit(solution)/shard_map/all_to_all | solution.py:15
  232.5 5.7 %reduce-scatter.2.cloned.1.call-done = bf16[128,256]{1,0:T(8,128)(2,1)} async-done(((bf16[4096,256]{1,0:T(8,128)(2,1)}), bf16[128,256]{1,0:T(8,128)(2,1)}) %reduce-scatter.2.cloned.1.call-update) | async-done | bytes 65552 | tf_op jit(solution)/shard_map/reduce_scatter | solution.py:156
  238.1 1.6 broadcast_in_dim.82
  239.7 4.1 %all-to-all-start.4 = ((bf16[4,128,256]{2,1,0:T(8,128)(2,1)}), bf16[4,128,256]{2,1,0:T(8,128)(2,1)S(1)}, u32[]{:S(2)}, u32[]{:S(2)}) async-start(bf16[4,128,256]{2,1,0:T(8,128)(2,1)} %broadcast_in_dim.82), calls=%async_computation.5 | async-start | bytes 524288 | tf_op jit(solution)/shard_map/all_to_all | solution.py:15
  243.8 2.3 fusion
  246.1 0.6 convert_reduce_fusion.3
  246.7 2.7 all-to-all-done.4
  249.4 0.7 convert_reduce_fusion.2
  250.0 31.5 %all-reduce.7.cloned.1.call-done = f32[256,256]{1,0:T(8,128)} async-done(((f32[256,256]{1,0:T(8,128)}), f32[256,256]{1,0:T(8,128)}) %all-reduce.7.cloned.1.call-update) | async-done | bytes 262160 | tf_op jit(solution)/shard_map/psum | solution.py:9
  281.6 1.7 copy.93
  (58 shorter events, 3.4 us)
Async XLA Ops:
  7.2 45.2 %copy-start = (bf16[4096,256]{1,0:T(8,128)(2,1)S(1)}, bf16[4096,256]{1,0:T(8,128)(2,1)}, u32[]{:S(2)}) copy-start(bf16[4096,256]{1,0:T(8,128)(2,1)} %param.21) | copy-start | bytes 6291460
  17.0 14.5 %copy-start.10 = (s32[64]{0:T(128)S(1)}, s32[64]{0:T(128)}, u32[]{:S(2)}) copy-start(s32[64]{0:T(128)} %param.14) | copy-start | bytes 772
  17.0 14.5 %copy-start.13 = (bf16[256]{0:T(256)(128)(2,1)S(1)}, bf16[256]{0:T(256)(128)(2,1)}, u32[]{:S(2)}) copy-start(bf16[256]{0:T(256)(128)(2,1)} %param.23) | copy-start | bytes 1540
  22.8 20.2 %all-to-all-start = ((bf16[32,2,4096]{2,1,0:T(2,128)(2,1)}), bf16[32,2,4096]{2,1,0:T(2,128)(2,1)S(1)}, u32[]{:S(2)}, u32[]{:S(2)}) async-start(bf16[32,2,4096]{2,1,0:T(2,128)(2,1)} %reshape.152), calls=%async_computation | async-start | bytes 1048576 | tf_op jit(solution)/shard_map/all_to_all | solution.py:146
  31.4 197.8 %all-reduce.5.cloned.1.call-start = ((), (), s32[]{:S(2)}) async-start(), calls=%async_computation.7 | async-start | bytes 524288 | tf_op jit(solution)/shard_map/psum | solution.py:9
  49.7 0.8 copy-start.9
  49.7 1.0 copy-start.12
  49.7 1.3 copy-start.8
  51.4 1.0 copy-start.5
  51.7 1.2 copy-start.3
  52.4 0.8 copy-start.7
  52.4 1.0 copy-start.11
  55.6 182.5 %reduce-scatter.2.cloned.1.call-start = ((), (), s32[]{:S(2)}) async-start(), calls=%async_computation.6 | async-start | bytes 2162688 | tf_op jit(solution)/shard_map/reduce_scatter | solution.py:156
  61.4 10.5 %all-to-all-start.1 = ((f32[32,1,128]{2,1,0:T(1,128)}), f32[32,1,128]{2,1,0:T(1,128)S(1)}, u32[]{:S(2)}, u32[]{:S(2)}) async-start(f32[32,1,128]{2,1,0:T(1,128)} %broadcast_in_dim.45), calls=%async_computation.1 | async-start | bytes 32768 | tf_op jit(solution)/shard_map/all_to_all | solution.py:15
  65.1 2.9 copy-start.1
  65.1 3.1 %copy-start.6 = (f32[64,128,32]{1,2,0:T(8,128)S(1)}, f32[64,128,32]{1,2,0:T(8,128)}, u32[]{:S(2)}) copy-start(f32[64,128,32]{1,2,0:T(8,128)} %copy-done.5) | copy-start | bytes 3145732
  67.9 1.3 copy-start.4
  72.0 149.9 %all-to-all-start.2 = ((bf16[64,128,32]{1,2,0:T(8,128)(2,1)}), bf16[64,128,32]{1,2,0:T(8,128)(2,1)S(1)}, u32[]{:S(2)}, u32[]{:S(2)}) async-start(bf16[64,128,32]{1,2,0:T(8,128)(2,1)} %gather_fusion.3), calls=%async_computation.2 | async-start | bytes 1048576 | tf_op jit(solution)/shard_map/all_to_all | solution.py:151
  78.7 1.9 copy-start.2
  224.7 7.7 %all-to-all-start.3 = ((bf16[4,2,128,32]{2,3,1,0:T(8,128)(2,1)}), bf16[4,2,128,32]{2,3,1,0:T(8,128)(2,1)S(1)}, u32[]{:S(2)}, u32[]{:S(2)}) async-start(bf16[4,2,128,32]{2,3,1,0:T(8,128)(2,1)} %broadcast_in_dim.49), calls=%async_computation.3 | async-start | bytes 131072 | tf_op jit(solution)/shard_map/all_to_all | solution.py:15
  228.0 53.6 %all-reduce.7.cloned.1.call-start = ((), (), s32[]{:S(2)}) async-start(), calls=%async_computation.8 | async-start | bytes 524288 | tf_op jit(solution)/shard_map/psum | solution.py:9
  239.7 9.7 %all-to-all-start.4 = ((bf16[4,128,256]{2,1,0:T(8,128)(2,1)}), bf16[4,128,256]{2,1,0:T(8,128)(2,1)S(1)}, u32[]{:S(2)}, u32[]{:S(2)}) async-start(bf16[4,128,256]{2,1,0:T(8,128)(2,1)} %broadcast_in_dim.82), calls=%async_computation.5 | async-start | bytes 524288 | tf_op jit(solution)/shard_map/all_to_all | solution.py:15
Sparse Core Ops, SparseCore 0:
  55.8 101.8 all-reduce.4
  161.2 76.8 reduce-scatter.1
  240.5 41.0 all-reduce.6
